TPU v7x, 32 devices: a whole 2x2x4 slice. The times are simulated.
32 devices in a mesh: spec: 8 (over z, y), wave: 4 (over x, core).
Axes of the slice: x: 2, y: 2, z: 4, core: 2. Of those that a mesh axis runs over, the one named last changes fastest.
Arguments:
- observed_flux: bfloat16 [2048, 2048], P('spec', 'wave'), may hold values from -6 to 6
- continuum_coeffs: bfloat16 [2048, 16], P('spec'), may hold values from -6 to 6
- continuum_basis: bfloat16 [16, 2048], P(None, 'wave'), may hold values from -1.5 to 1.5
- centres: int32 [2048, 16], P('spec', 'wave'), may hold values from 0 to 2047, as said below
- line_index: int32 [2048, 16], P('spec', 'wave'), may hold values from 0 to 31
- column_factor: float32 [2048, 16], P('spec', 'wave'), may hold values from 0.3 to 3
- wing_width: int32 [2048], P('spec'), may hold values from 8 to 32, as said below
- line_strength: float32 [32], replicated, may hold values from 0.2 to 2
- line_widths: float32 [32], replicated, may hold values from 1 to 6
- sketch_matrix: bfloat16 [2048, 512], P('wave'), may hold values from -0.125 to 0.125
Outputs:
- residual: bfloat16 [2048, 2048], P('spec', 'wave')
- rfactor: float32 [512, 512], replicated
Inputs may be any that keep to these rules, and one draw needn't show every extreme that they name: The absorbers in columns k * 4 to (k + 1) * 4 - 1 have centres in pixels k * 512 to (k + 1) * 512 - 1; spectrum 0 has absorbers at pixel 0 and at pixel 2048 - 1. `wing_width`: spectrum 0 has the largest half-width.
All inputs are finite; a program needn't handle non-finite values.
Results may differ from a plain program's by a relative error of at most 0.0026.
Values sent between devices are 32-bit elements; how exact they have to be, the bound alone decides.
No kernel may reach another device: no remote copies, remote signals or barrier semaphores. Data moves between devices by JAX's collectives and lax.ppermute only.
A program may use at most 64 MiB of HBM per device.

v0:
```python
import jax
import jax.numpy as jnp
from jax import lax
from jax.sharding import PartitionSpec as P

WING = 32
voigt_mix = 0.5
log_two = 0.6931471805599453


def extended_2(block, sides, width):
    for axis, dim in sides:
        count = lax.axis_size(axis)
        forward = [(i, i + 1) for i in range(count - 1)]
        backward = [(target, source) for source, target in forward]
        low = lax.ppermute(
            lax.slice_in_dim(block, block.shape[dim] - width, None, axis=dim), axis, forward
        )
        high = lax.ppermute(lax.slice_in_dim(block, 0, width, axis=dim), axis, backward)
        block = jnp.concatenate([low, block, high], axis=dim)
    return block


def profile(offset, amplitude, inverse_width, wing_limit):
    scaled = offset * inverse_width
    values = amplitude * (
        voigt_mix / (1.0 + scaled * scaled)
        + (1.0 - voigt_mix) * jnp.exp(-log_two * scaled * scaled)
    )
    return jnp.where(jnp.abs(offset) <= wing_limit, values, 0.0)


def windowed_depth(centre_int, amplitude, inverse_width, wing_limit, anchor, width):
    pixels = anchor + jnp.arange(width, dtype=jnp.int32)
    offset_int = pixels[None, None, :] - centre_int[:, :, None]
    offset_float = offset_int.astype(jnp.float32)
    values = profile(
        offset_float, amplitude[:, :, None], inverse_width[:, :, None], wing_limit[:, :, None]
    )
    return jnp.sum(values, axis=1)


def shards(
    observed_flux,
    continuum_coeffs,
    continuum_basis,
    centres,
    line_index,
    column_factor,
    wing_width,
    line_strength,
    line_widths,
    sketch_matrix,
):
    spectra, pix_local = observed_flux.shape
    first_pixel = lax.axis_index("wave") * pix_local
    onehot = (
        line_index[:, :, None] == jnp.arange(line_strength.shape[0], dtype=jnp.int32)[None, None, :]
    ).astype(jnp.float32)
    amplitude = column_factor * jnp.sum(onehot * line_strength, axis=2)
    inverse_width = 1.0 / jnp.sum(onehot * line_widths, axis=2)
    wing_limit = wing_width.astype(jnp.float32)[:, None]
    extended = windowed_depth(
        centres, amplitude, inverse_width, wing_limit, first_pixel - WING, pix_local + 2 * WING
    )
    outgoing = jnp.concatenate([extended[:, :WING], extended[:, -WING:]], axis=1)
    padded_rims = extended_2(outgoing, (("wave", 1),), WING)
    optical_depth = extended[:, WING:-WING]
    optical_depth = optical_depth.at[:, :WING].add(padded_rims[:, :WING])
    optical_depth = optical_depth.at[:, -WING:].add(padded_rims[:, 3 * WING :])
    continuum = jnp.dot(continuum_coeffs, continuum_basis, preferred_element_type=jnp.float32)
    residual = (observed_flux.astype(jnp.float32) - continuum * jnp.exp(-optical_depth)).astype(
        jnp.bfloat16
    )
    spectra_total = spectra * lax.axis_size("spec")
    partial_sketch = jnp.dot(residual, sketch_matrix, preferred_element_type=jnp.float32)
    sketch = lax.psum(partial_sketch, "wave")
    local_gram = jnp.dot(
        sketch.T, sketch, precision=lax.Precision.HIGHEST, preferred_element_type=jnp.float32
    )
    gram_matrix = lax.psum(local_gram, "spec")
    gram_matrix = gram_matrix / spectra_total
    rfactor = jnp.linalg.cholesky(gram_matrix).T
    return (residual, rfactor)


def solution(mesh):
    return jax.shard_map(
        shards,
        mesh=mesh,
        in_specs=(
            P("spec", "wave"),
            P("spec", None),
            P(None, "wave"),
            P("spec", "wave"),
            P("spec", "wave"),
            P("spec", "wave"),
            P("spec"),
            P(),
            P(),
            P("wave", None),
        ),
        out_specs=(P("spec", "wave"), P()),
        check_vma=False,
    )
```

profile of v0, /device:TPU:0, one launch (start us, length us, event | category | flops | bytes accessed | tf_op | source)
XLA Modules:
  0.0 237.7 jit_solution(6965424051535711169)
XLA Ops:
  7.2 0.0 copy-start
  7.2 0.0 all-reduce.4.cloned.1.call-start
  7.2 0.7 convert_element_type.15
  8.0 0.8 select_reduce_fusion.1
  8.8 0.7 mul.59
  9.5 2.2 fusion.5
  11.7 0.1 copy.28
  11.8 2.4 collective-permute-start
  14.2 0.1 copy.29
  14.3 1.3 collective-permute-start.1
  15.6 0.0 copy-start.5
  15.7 0.0 copy-start.6
  15.7 0.0 copy-start.7
  15.7 0.2 copy.26
  15.9 0.1 copy.27
  16.0 0.6 compare_reduce_fusion.4
  16.6 0.0 collective-permute-done
  16.6 0.7 add_select_fusion
  17.3 1.1 scatter-add.6
  18.4 1.3 collective-permute-done.1
  19.6 0.1 slice_add_fusion
  19.7 0.9 scatter-add.9
  20.6 0.0 copy-done.5
  20.7 0.0 copy-done.6
  20.7 0.0 copy-done.7
  20.7 0.2 subtract_convert_fusion
  20.9 0.0 copy-done
  20.9 0.0 copy-start.4
  20.9 1.1 fusion.19
  22.0 0.0 all-reduce.4.cloned.1.call-update
  22.1 0.2 all-reduce.6.cloned.1.call-start
  22.3 36.6 %all-reduce.4.cloned.1.call-done = f32[256,512]{1,0:T(8,128)} async-done(((f32[256,512]{1,0:T(8,128)}), f32[256,512]{1,0:T(8,128)}) %all-reduce.4.cloned.1.call-update) | async-done | bytes 524304 | tf_op jit(solution)/shard_map/psum | solution.py:77
  58.9 3.2 %fusion.20 = f32[512,512]{0,1:T(8,128)} fusion(f32[256,512]{1,0:T(8,128)} %all-reduce.4.cloned.1.call-done), kind=kOutput, calls=%fused_computation.57 | convolution fusion | flops 805306368 | bytes 1572864 | tf_op jit(solution)/shard_map/dot_general | solution.py:78
  62.2 0.0 copy-done.4
  62.2 0.0 all-reduce.6.cloned.1.call-update
  62.2 78.9 %all-reduce.6.cloned.1.call-done = f32[512,512]{0,1:T(8,128)} async-done(((f32[512,512]{0,1:T(8,128)}), f32[512,512]{0,1:T(8,128)}) %all-reduce.6.cloned.1.call-update) | async-done | bytes 1048592 | tf_op jit(solution)/shard_map/psum | solution.py:81
  141.0 2.3 broadcast_multiply_fusion
  143.3 0.0 copy-start.1
  143.3 1.6 copy.23
  145.0 0.0 copy-done.1
  145.0 0.2 fusion.6
  145.2 0.0 copy-start.2
  145.3 1.0 copy-done.2
  146.2 0.0 copy-start.3
  146.2 11.7 %cholesky.104 = f32[128,128]{1,0:T(8,128)S(1)} custom-call(f32[128,128]{1,0:T(8,128)S(1)} %cholesky.266), custom_call_target="Cholesky" | custom-call | tf_op jit(solution)/shard_map/jit(cholesky)/cholesky | solution.py:83
  158.0 9.8 %custom-call.27 = f32[1,128,128]{1,2,0:T(8,128)S(1)} custom-call(f32[1,128,128]{2,1,0:T(8,128)S(1)} %get-tuple-element.44), custom_call_target="InvertDiagBlocksLowerTriangular" | custom-call | tf_op jit(solution)/shard_map/jit(cholesky)/cholesky | solution.py:83
  167.8 0.1 cholesky.224
  167.9 0.0 copy-done.3
  167.9 0.3 constant_dynamic-update-slice_fusion.2
  168.3 0.3 convolution_subtract_fusion
  168.6 11.8 %cholesky.217 = f32[128,128]{1,0:T(8,128)S(1)} custom-call(f32[128,128]{1,0:T(8,128)S(1)} %cholesky.270), custom_call_target="Cholesky" | custom-call | tf_op jit(solution)/shard_map/jit(cholesky)/cholesky | solution.py:83
  180.5 9.8 %custom-call.28 = f32[1,128,128]{1,2,0:T(8,128)S(1)} custom-call(f32[1,128,128]{2,1,0:T(8,128)S(1)} %get-tuple-element.41), custom_call_target="InvertDiagBlocksLowerTriangular" | custom-call | tf_op jit(solution)/shard_map/jit(cholesky)/cholesky | solution.py:83
  190.3 0.3 convolution_dynamic-update-slice_fusion
  190.6 0.4 convolution_subtract_fusion.1
  191.0 11.7 %cholesky.238 = f32[128,128]{1,0:T(8,128)S(1)} custom-call(f32[128,128]{1,0:T(8,128)S(1)} %cholesky.275), custom_call_target="Cholesky" | custom-call | tf_op jit(solution)/shard_map/jit(cholesky)/cholesky | solution.py:83
  202.7 0.7 compare_reduce_fusion.1
  203.4 9.8 %custom-call.29 = f32[1,128,128]{1,2,0:T(8,128)S(1)} custom-call(f32[1,128,128]{2,1,0:T(8,128)S(1)} %get-tuple-element.38), custom_call_target="InvertDiagBlocksLowerTriangular" | custom-call | tf_op jit(solution)/shard_map/jit(cholesky)/cholesky | solution.py:83
  213.3 0.2 convolution_dynamic-update-slice_fusion.1
  213.5 0.4 convolution_subtract_fusion.2
  213.9 11.7 %cholesky.255 = f32[128,128]{1,0:T(8,128)S(1)} custom-call(f32[128,128]{1,0:T(8,128)S(1)} %convolution_subtract_fusion.2), custom_call_target="Cholesky" | custom-call | tf_op jit(solution)/shard_map/jit(cholesky)/cholesky | solution.py:83
  225.6 0.6 compare_reduce_fusion
  226.2 0.7 compare_reduce_fusion.2
  229.4 0.1 select_bitcast_fusion
  229.6 1.3 copy.24
  (11 shorter events, 0.2 us)
Async XLA Ops:
  7.2 13.8 %copy-start = (bf16[512,512]{1,0:T(8,128)(2,1)S(1)}, bf16[512,512]{1,0:T(8,128)(2,1)}, u32[]{:S(2)}) copy-start(bf16[512,512]{1,0:T(8,128)(2,1)} %param.23) | copy-start | bytes 1572868
  7.2 51.8 %all-reduce.4.cloned.1.call-start = ((), (), s32[]{:S(2)}) async-start(), calls=%async_computation | async-start | bytes 1048576 | tf_op jit(solution)/shard_map/psum | solution.py:77
  11.8 4.8 %collective-permute-start = (f32[256,32]{1,0:T(8,128)S(1)}, f32[256,32]{1,0:T(8,128)S(1)}, u32[]{:S(2)}, u32[]{:S(2)}) collective-permute-start(f32[256,32]{1,0:T(8,128)S(1)} %copy.28), channel_id=1, source_target_pairs={{0,1},{1,2},{2,3},{4,5},{5,6},{6,7},{8,9},{9,10},{10,11},{12,13},{... | collective-permute-start | bytes 98312 | tf_op jit(solution)/shard_map/ppermute | solution.py:16
  14.3 5.3 %collective-permute-start.1 = (f32[256,32]{1,0:T(8,128)S(1)}, f32[256,32]{1,0:T(8,128)S(1)}, u32[]{:S(2)}, u32[]{:S(2)}) collective-permute-start(f32[256,32]{1,0:T(8,128)S(1)} %copy.29), channel_id=1, source_target_pairs={{1,0},{2,1},{3,2},{5,4},{6,5},{7,6},{9,8},{10,9},{11,10},{13,12},{... | collective-permute-start | bytes 98312 | tf_op jit(solution)/shard_map/ppermute | solution.py:19
  15.6 5.0 %copy-start.5 = (bf16[256,512]{1,0:T(8,128)(2,1)S(1)}, bf16[256,512]{1,0:T(8,128)(2,1)}, u32[]{:S(2)}) copy-start(bf16[256,512]{1,0:T(8,128)(2,1)} %param.14) | copy-start | bytes 786436
  15.7 5.0 %copy-start.6 = (bf16[16,512]{1,0:T(8,128)(2,1)S(1)}, bf16[16,512]{1,0:T(8,128)(2,1)}, u32[]{:S(2)}) copy-start(bf16[16,512]{1,0:T(8,128)(2,1)} %param.16) | copy-start | bytes 49156
  15.7 5.0 %copy-start.7 = (bf16[256,16]{0,1:T(8,128)(2,1)S(1)}, bf16[256,16]{0,1:T(8,128)(2,1)}, u32[]{:S(2)}) copy-start(bf16[256,16]{0,1:T(8,128)(2,1)} %param.15) | copy-start | bytes 24580
  20.9 41.2 %copy-start.4 = (bf16[256,512]{1,0:T(8,128)(2,1)}, bf16[256,512]{1,0:T(8,128)(2,1)S(1)}, u32[]{:S(2)}) copy-start(bf16[256,512]{1,0:T(8,128)(2,1)S(1)} %subtract_convert_fusion) | copy-start | bytes 786436
  22.1 119.0 %all-reduce.6.cloned.1.call-start = ((), (), s32[]{:S(2)}) async-start(), calls=%async_computation.1 | async-start | bytes 2097152 | tf_op jit(solution)/shard_map/psum | solution.py:81
  143.3 1.7 copy-start.1
  145.2 1.0 copy-start.2
  146.2 21.7 %copy-start.3 = (f32[512,512]{1,0:T(8,128)S(1)}, f32[512,512]{1,0:T(8,128)}, u32[]{:S(2)}) copy-start(f32[512,512]{1,0:T(8,128)} %copy-done.2) | copy-start | bytes 3145732
Sparse Core Ops, SparseCore 0:
  22.2 36.7 all-reduce.3
  63.0 77.9 all-reduce.5
where the time goes:
time: 238 us
  waiting for transfers between devices  117 us (49%)
  other arithmetic  87.1 us (37%)
  between operations  16.9 us (7%)
  local copies, waits for them, and re-layouts  6.6 us (3%)
  matrix products  6.44 us (3%)
  starting transfers between devices  3.91 us (2%)
    psum x1, waiting for transfers between devices, shards(): gram_matrix = lax.psum(local_gram, 'spec')  78.9 us
    another operation x14, other arithmetic, shards(): rfactor = jnp.linalg.cholesky(gram_matrix).T  78.6 us
    psum x1, waiting for transfers between devices, shards(): sketch = lax.psum(partial_sketch, 'wave')  36.6 us
  transfers between devices with their start and end apart: 4, of which 3 were waited for; matrix products, arithmetic and copies ran while one was open for 1% of the time, Pallas kernels for 0%

commit v1 on v0

--- a/solution.py
+++ b/solution.py
@@ -78,7 +78,7 @@
     local_gram = jnp.dot(
         sketch.T, sketch, precision=lax.Precision.HIGHEST, preferred_element_type=jnp.float32
     )
-    gram_matrix = lax.psum(local_gram, "spec")
+    gram_matrix = jnp.sum(lax.all_gather(local_gram, "spec"), axis=0)
     gram_matrix = gram_matrix / spectra_total
     rfactor = jnp.linalg.cholesky(gram_matrix).T
     return (residual, rfactor)

time: 238 us -> 289 us (1.21)
  waiting for transfers between devices: 117 us -> 163 us
  matrix products: 6.44 us -> 10 us
    all_gather x0 -> x1, waiting for transfers between devices: none -> 125 us  [shards(): gram_matrix = jnp.sum(lax.all_gather(local_gram, 'spec'), axis=0)]
    psum x1 -> x0, waiting for transfers between devices: 78.9 us -> none  [shards(): gram_matrix = lax.psum(local_gram, 'spec')]
    reduce_sum x0 -> x1, other arithmetic: none -> 4.49 us  [shards(): gram_matrix = jnp.sum(lax.all_gather(local_gram, 'spec'), axis=0)]
    another operation x6, matrix products: 1.87 us -> 5.46 us  [shards(): rfactor = jnp.linalg.cholesky(gram_matrix).T]
where the time goes in v1:
time: 289 us
  waiting for transfers between devices  163 us (56%)
  other arithmetic  89.6 us (31%)
  between operations  16.9 us (6%)
  matrix products  10 us (3%)
  local copies, waits for them, and re-layouts  5.27 us (2%)
  starting transfers between devices  3.91 us (1%)
    all_gather x1, waiting for transfers between devices, shards(): gram_matrix = jnp.sum(lax.all_gather(local_gram, 'spec'), axis=0)  125 us
    another operation x14, other arithmetic, shards(): rfactor = jnp.linalg.cholesky(gram_matrix).T  78.9 us
    psum x1, waiting for transfers between devices, shards(): sketch = lax.psum(partial_sketch, 'wave')  36.6 us
  transfers between devices with their start and end apart: 4, of which 3 were waited for; matrix products, arithmetic and copies ran while one was open for 1% of the time, Pallas kernels for 0%

profile of v1, /device:TPU:0, one launch (start us, length us, event | category | flops | bytes accessed | tf_op | source)
XLA Modules:
  0.0 288.7 jit_solution(16279065981346914174)
XLA Ops:
  7.2 0.0 copy-start
  7.2 0.0 all-reduce.3.cloned.1.call-start
  7.2 0.7 convert_element_type.15
  8.0 0.8 select_reduce_fusion.1
  8.8 0.7 mul.59
  9.5 0.0 copy-start.3
  9.5 0.0 copy-start.4
  9.5 0.0 copy-start.5
  9.5 2.3 fusion.5
  11.8 0.1 copy.30
  11.9 2.4 collective-permute-start
  14.2 0.1 copy.31
  14.3 1.3 collective-permute-start.1
  15.7 0.2 copy.28
  15.9 0.1 copy.29
  16.0 0.6 compare_reduce_fusion.4
  16.6 0.0 collective-permute-done
  16.6 0.7 add_select_fusion
  17.3 1.1 scatter-add.6
  18.4 1.3 collective-permute-done.1
  19.7 0.1 slice_add_fusion
  19.8 0.9 scatter-add.9
  20.7 0.0 copy-done.3
  20.7 0.0 copy-done.4
  20.7 0.0 copy-done.5
  20.7 0.3 subtract_convert_fusion
  21.0 0.0 copy-done
  21.0 0.0 copy-start.2
  21.0 1.1 fusion.19
  22.1 0.0 all-reduce.3.cloned.1.call-update
  22.1 0.2 all-gather.3.cloned.1.call-start
  22.3 36.6 %all-reduce.3.cloned.1.call-done = f32[256,512]{1,0:T(8,128)} async-done(((f32[256,512]{1,0:T(8,128)}), f32[256,512]{1,0:T(8,128)}) %all-reduce.3.cloned.1.call-update) | async-done | bytes 524304 | tf_op jit(solution)/shard_map/psum | solution.py:77
  59.0 3.2 %fusion.20 = f32[512,512]{1,0:T(8,128)} fusion(f32[256,512]{1,0:T(8,128)} %all-reduce.3.cloned.1.call-done), kind=kOutput, calls=%fused_computation.56 | convolution fusion | flops 805306368 | bytes 1572864 | tf_op jit(solution)/shard_map/dot_general | solution.py:78
  62.2 0.0 all-gather.3.cloned.1.call-update
  62.2 0.0 copy-done.2
  62.2 125.1 %all-gather.3.cloned.1.call-done = f32[4096,512]{1,0:T(8,128)} async-done(((f32[512,512]{1,0:T(8,128)}), f32[4096,512]{1,0:T(8,128)}) %all-gather.3.cloned.1.call-update) | async-done | bytes 8388624 | tf_op jit(solution)/shard_map/all_gather | solution.py:81
  187.3 4.5 %reduce_sum.41 = f32[512,512]{1,0:T(8,128)S(1)} reduce(f32[8,512,512]{2,1,0:T(8,128)} %bitcast.31, f32[]{:T(128)} %constant.201.clone.1), dimensions={0}, to_apply=%region_5.6 | reduce | flops 1835008 | bytes 9437188 | tf_op jit(solution)/shard_map/reduce_sum | solution.py:81
  191.8 0.3 copy.26
  192.1 0.2 fusion.6
  192.4 0.0 copy-start.1
  192.4 1.0 copy-done.1
  193.4 11.7 %cholesky.104 = f32[128,128]{1,0:T(8,128)S(1)} custom-call(f32[128,128]{1,0:T(8,128)S(1)} %cholesky.266), custom_call_target="Cholesky" | custom-call | tf_op jit(solution)/shard_map/jit(cholesky)/cholesky | solution.py:83
  205.1 0.1 cholesky.224
  205.2 9.8 %custom-call.27 = f32[1,128,128]{1,2,0:T(8,128)S(1)} custom-call(f32[1,128,128]{2,1,0:T(8,128)S(1)} %get-tuple-element.46), custom_call_target="InvertDiagBlocksLowerTriangular" | custom-call | tf_op jit(solution)/shard_map/jit(cholesky)/cholesky | solution.py:83
  215.0 1.2 constant_dynamic-update-slice_fusion.2
  216.3 1.3 convolution_subtract_fusion
  217.6 11.9 %cholesky.217 = f32[128,128]{1,0:T(8,128)S(1)} custom-call(f32[128,128]{1,0:T(8,128)S(1)} %cholesky.270), custom_call_target="Cholesky" | custom-call | tf_op jit(solution)/shard_map/jit(cholesky)/cholesky | solution.py:83
  229.5 9.8 %custom-call.28 = f32[1,128,128]{1,2,0:T(8,128)S(1)} custom-call(f32[1,128,128]{2,1,0:T(8,128)S(1)} %get-tuple-element.43), custom_call_target="InvertDiagBlocksLowerTriangular" | custom-call | tf_op jit(solution)/shard_map/jit(cholesky)/cholesky | solution.py:83
  239.3 0.3 convolution_dynamic-update-slice_fusion
  239.6 1.3 convolution_subtract_fusion.1
  240.9 11.7 %cholesky.238 = f32[128,128]{1,0:T(8,128)S(1)} custom-call(f32[128,128]{1,0:T(8,128)S(1)} %cholesky.275), custom_call_target="Cholesky" | custom-call | tf_op jit(solution)/shard_map/jit(cholesky)/cholesky | solution.py:83
  252.7 0.7 compare_reduce_fusion.1
  253.4 9.8 %custom-call.29 = f32[1,128,128]{1,2,0:T(8,128)S(1)} custom-call(f32[1,128,128]{2,1,0:T(8,128)S(1)} %get-tuple-element.40), custom_call_target="InvertDiagBlocksLowerTriangular" | custom-call | tf_op jit(solution)/shard_map/jit(cholesky)/cholesky | solution.py:83
  263.2 0.2 convolution_dynamic-update-slice_fusion.1
  263.4 1.2 convolution_subtract_fusion.2
  264.6 11.9 %cholesky.255 = f32[128,128]{1,0:T(8,128)S(1)} custom-call(f32[128,128]{1,0:T(8,128)S(1)} %convolution_subtract_fusion.2), custom_call_target="Cholesky" | custom-call | tf_op jit(solution)/shard_map/jit(cholesky)/cholesky | solution.py:83
  276.6 0.6 compare_reduce_fusion
  277.2 0.7 compare_reduce_fusion.2
  280.4 0.1 select_bitcast_fusion
  280.6 1.3 copy.27
  (11 shorter events, 0.2 us)
Async XLA Ops:
  7.2 13.8 %copy-start = (bf16[512,512]{1,0:T(8,128)(2,1)S(1)}, bf16[512,512]{1,0:T(8,128)(2,1)}, u32[]{:S(2)}) copy-start(bf16[512,512]{1,0:T(8,128)(2,1)} %param.23) | copy-start | bytes 1572868
  7.2 51.8 %all-reduce.3.cloned.1.call-start = ((), (), s32[]{:S(2)}) async-start(), calls=%async_computation | async-start | bytes 1048576 | tf_op jit(solution)/shard_map/psum | solution.py:77
  9.5 11.2 %copy-start.3 = (bf16[256,512]{1,0:T(8,128)(2,1)S(1)}, bf16[256,512]{1,0:T(8,128)(2,1)}, u32[]{:S(2)}) copy-start(bf16[256,512]{1,0:T(8,128)(2,1)} %param.14) | copy-start | bytes 786436
  9.5 11.2 %copy-start.4 = (bf16[16,512]{1,0:T(8,128)(2,1)S(1)}, bf16[16,512]{1,0:T(8,128)(2,1)}, u32[]{:S(2)}) copy-start(bf16[16,512]{1,0:T(8,128)(2,1)} %param.16) | copy-start | bytes 49156
  9.5 11.2 %copy-start.5 = (bf16[256,16]{0,1:T(8,128)(2,1)S(1)}, bf16[256,16]{0,1:T(8,128)(2,1)}, u32[]{:S(2)}) copy-start(bf16[256,16]{0,1:T(8,128)(2,1)} %param.15) | copy-start | bytes 24580
  11.9 4.8 %collective-permute-start = (f32[256,32]{1,0:T(8,128)S(1)}, f32[256,32]{1,0:T(8,128)S(1)}, u32[]{:S(2)}, u32[]{:S(2)}) collective-permute-start(f32[256,32]{1,0:T(8,128)S(1)} %copy.30), channel_id=1, source_target_pairs={{0,1},{1,2},{2,3},{4,5},{5,6},{6,7},{8,9},{9,10},{10,11},{12,13},{... | collective-permute-start | bytes 98312 | tf_op jit(solution)/shard_map/ppermute | solution.py:16
  14.3 5.3 %collective-permute-start.1 = (f32[256,32]{1,0:T(8,128)S(1)}, f32[256,32]{1,0:T(8,128)S(1)}, u32[]{:S(2)}, u32[]{:S(2)}) collective-permute-start(f32[256,32]{1,0:T(8,128)S(1)} %copy.31), channel_id=1, source_target_pairs={{1,0},{2,1},{3,2},{5,4},{6,5},{7,6},{9,8},{10,9},{11,10},{13,12},{... | collective-permute-start | bytes 98312 | tf_op jit(solution)/shard_map/ppermute | solution.py:19
  21.0 41.2 %copy-start.2 = (bf16[256,512]{1,0:T(8,128)(2,1)}, bf16[256,512]{1,0:T(8,128)(2,1)S(1)}, u32[]{:S(2)}) copy-start(bf16[256,512]{1,0:T(8,128)(2,1)S(1)} %subtract_convert_fusion) | copy-start | bytes 786436
  22.1 165.2 %all-gather.3.cloned.1.call-start = ((), (), s32[]{:S(2)}) async-start(), calls=%async_computation.1 | async-start | bytes 9437184 | tf_op jit(solution)/shard_map/all_gather | solution.py:81
  192.4 1.0 copy-start.1
Sparse Core Ops, SparseCore 0:
  22.2 36.7 all-reduce.2
  62.3 124.9 all-gather.2
